TPU v7x, 256 devices: a whole 4x4x8 slice. The times are simulated.
256 devices in a mesh: dp: 8 (over z), expert: 8 (over x, core), tensor: 4 (over y).
Axes of the slice: x: 4, y: 4, z: 8, core: 2. Of those that a mesh axis runs over, the one named last changes fastest.
Arguments:
- skip_stream_entry: bfloat16 [4096, 4096], P(('dp', 'expert', 'tensor')), may hold values from -6 to 6
- question_vectors: bfloat16 [4096, 2048], P(('dp', 'expert'), 'tensor'), may hold values from -5 to 5
- fresh_lookup_vectors: bfloat16 [4096, 512], P(('dp', 'expert'), 'tensor'), may hold values from -5 to 5
- fresh_content_vectors: bfloat16 [4096, 512], P(('dp', 'expert'), 'tensor'), may hold values from -10 to 10
- stored_lookup_sheets: bfloat16 [2560, 4, 128, 128], P(('dp', 'expert'), 'tensor'), may hold values from -5 to 5
- stored_content_sheets: bfloat16 [2560, 4, 128, 128], P(('dp', 'expert'), 'tensor'), may hold values from -10 to 10
- sequence_sheet_map: int32 [1088, 8], P(('dp', 'expert')), may hold values from 0 to 39
- stored_position_counts: int32 [1088], P(('dp', 'expert')), may hold values from 2 to 1024
- attention_merge_matrix: bfloat16 [2048, 4096], P('tensor'), may hold values from -0.59765625 to 0.59765625
- premix_scale_factor: bfloat16 [4096], replicated, may hold values from 0.5 to 1.5
- chosen_specialists: int32 [4096, 2], P(('dp', 'expert', 'tensor')), may hold values from 0 to 7, all different within a row; in each aligned block of 16 rows (0 to 15, 16 to 31, ...) at most 6 rows name the same one
- selection_shares: float32 [4096, 2], P(('dp', 'expert', 'tensor')), may hold values from 0.2 to 1
- allowed_placements: int32 [8], replicated, may hold values from 2 to 3
- favored_specialist: int32 [1], replicated, may hold values from 0 to 7
- gating_matrices: bfloat16 [8, 7168, 4096], P('expert', ('dp', 'tensor')), may hold values from -0.09375 to 0.09375
- expand_matrices: bfloat16 [8, 7168, 4096], P('expert', ('dp', 'tensor')), may hold values from -0.09375 to 0.09375
- contract_matrices: bfloat16 [8, 7168, 4096], P('expert', ('dp', 'tensor')), may hold values from -0.0625 to 0.0625
Outputs:
- layer_out: bfloat16 [4096, 4096], P(('dp', 'expert', 'tensor'))
Inputs may be any that keep to these rules, and one draw needn't show every extreme that they name: `chosen_specialists`: in the 16 rows of one device no expert is named by more than 6 rows; a token names two different experts.
All inputs are finite; a program needn't handle non-finite values.
Results may differ from a plain program's by a relative error of at most 0.018.
Values may be sent and summed in bfloat16 or wider, within the bound.
A program may use at most 128 MiB of HBM per device.

v0:
```python
from functools import reduce
import math
import jax
import jax.numpy as jnp
from jax import lax
from jax.sharding import PartitionSpec as P

HD = 128
PLACEMENT_MOST = 6


def normalize(parts):
    highest = reduce(
        jnp.maximum,
        [
            jnp.max(jnp.where(visible, scores, -jnp.inf), axis=-1, keepdims=True)
            for scores, visible in parts
        ],
    )
    portions = [jnp.where(visible, jnp.exp(scores - highest), 0.0) for scores, visible in parts]
    denominator = reduce(
        jnp.add, [jnp.sum(portion, axis=-1, keepdims=True) for portion in portions]
    )
    return [(portion / denominator).astype(jnp.bfloat16) for portion in portions]


def attend(question_vectors, new_keys, new_values, key_pages, value_pages, table, spans):
    rows_all, head_count, head_width = question_vectors.shape
    kv_heads = new_keys.shape[1]
    group_size = head_count // kv_heads
    single_count = spans.shape[0] - 1
    page_count = table.shape[1]
    page_width = key_pages.shape[2]
    context = page_count * page_width
    inverse_root = 1.0 / math.sqrt(head_width)
    page_keys = key_pages[table]
    page_values = value_pages[table]
    grouped = question_vectors.reshape(rows_all, kv_heads, group_size, head_width)
    positions = jnp.arange(context, dtype=jnp.int32)
    single_q = grouped[:single_count]
    cache_dec = (
        jnp.einsum(
            "rkgh,rmkph->rkgmp",
            single_q,
            page_keys[:single_count],
            preferred_element_type=jnp.float32,
        ).reshape(single_count, kv_heads, group_size, context)
        * inverse_root
    )
    seen_dec = (positions[None, :] < spans[:single_count, None])[:, None, None, :]
    own_dec = (
        jnp.einsum(
            "rkgh,rkh->rkg", single_q, new_keys[:single_count], preferred_element_type=jnp.float32
        )[..., None]
        * inverse_root
    )
    weight_cache, weight_own = normalize(
        [(cache_dec, seen_dec), (own_dec, jnp.full(own_dec.shape, True))]
    )
    out_dec = jnp.einsum(
        "rkgmp,rmkph->rkgh",
        weight_cache.reshape(single_count, kv_heads, group_size, page_count, page_width),
        page_values[:single_count],
        preferred_element_type=jnp.float32,
    )
    out_dec = (
        out_dec
        + weight_own.astype(jnp.float32)
        * new_values[:single_count].astype(jnp.float32)[:, :, None, :]
    )
    prompt_q = grouped[single_count:]
    prompt_rows = rows_all - single_count
    cache_pro = (
        jnp.einsum(
            "rkgh,mkph->rkgmp",
            prompt_q,
            page_keys[single_count],
            preferred_element_type=jnp.float32,
        ).reshape(prompt_rows, kv_heads, group_size, context)
        * inverse_root
    )
    seen_pro = (positions < spans[single_count])[None, None, None, :]
    new_pro = (
        jnp.einsum(
            "rkgh,mkh->rkgm", prompt_q, new_keys[single_count:], preferred_element_type=jnp.float32
        )
        * inverse_root
    )
    prompt_index = jnp.arange(prompt_rows, dtype=jnp.int32)
    causal = (prompt_index[:, None] >= prompt_index[None, :])[:, None, None, :]
    weight_cpro, weight_npro = normalize([(cache_pro, seen_pro), (new_pro, causal)])
    out_pro = jnp.einsum(
        "rkgmp,mkph->rkgh",
        weight_cpro.reshape(prompt_rows, kv_heads, group_size, page_count, page_width),
        page_values[single_count],
        preferred_element_type=jnp.float32,
    )
    out_pro = out_pro + jnp.einsum(
        "rkgm,mkh->rkgh", weight_npro, new_values[single_count:], preferred_element_type=jnp.float32
    )
    joined = jnp.concatenate([out_dec, out_pro], axis=0).astype(jnp.bfloat16)
    return joined.reshape(rows_all, head_count * head_width)


def slot_table(member, ranking, keeping, slot_count):
    slot_hit = (
        ranking[:, :, None, None] == jnp.arange(slot_count, dtype=jnp.int32)[None, None, None, :]
    )
    return ((member[..., None] > 0) & keeping[:, :, None, None] & slot_hit).astype(jnp.bfloat16)


def expert_pass(send, gating_matrices, expand_matrices, contract_matrices):
    specialist_index, slot_count, model_width = send.shape
    holders = lax.axis_size("expert")
    local_count = gating_matrices.shape[0]
    arrived = lax.all_to_all(
        send.reshape(holders, local_count, slot_count, model_width),
        "expert",
        split_axis=0,
        concat_axis=0,
        tiled=True,
    )
    row_piece = lax.all_gather(arrived, ("dp", "tensor"), axis=0, tiled=True)
    gate_part = jnp.einsum(
        "qesd,efd->qesf", row_piece, gating_matrices, preferred_element_type=jnp.float32
    )
    up_part = jnp.einsum(
        "qesd,efd->qesf", row_piece, expand_matrices, preferred_element_type=jnp.float32
    )
    hidden = (jax.nn.silu(gate_part) * up_part).astype(jnp.bfloat16)
    summed = lax.psum_scatter(
        jnp.einsum(
            "qesf,efd->qesd", hidden, contract_matrices, preferred_element_type=jnp.float32
        ).astype(jnp.bfloat16),
        ("dp", "tensor"),
        scatter_dimension=0,
        tiled=True,
    )
    arrived_back = lax.all_to_all(summed, "expert", split_axis=0, concat_axis=0, tiled=True)
    return arrived_back.reshape(specialist_index, slot_count, model_width)


def local(
    skip_stream_entry,
    question_vectors,
    fresh_lookup_vectors,
    fresh_content_vectors,
    stored_lookup_sheets,
    stored_content_sheets,
    sequence_sheet_map,
    stored_position_counts,
    attention_merge_matrix,
    premix_scale_factor,
    chosen_specialists,
    selection_shares,
    allowed_placements,
    favored_specialist,
    gating_matrices,
    expand_matrices,
    contract_matrices,
):
    token_count = chosen_specialists.shape[0]
    specialist_index = allowed_placements.shape[0]
    picked = (
        chosen_specialists[:, :, None]
        == jnp.arange(specialist_index, dtype=jnp.int32)[None, None, :]
    ).astype(jnp.int32)
    flat_routes = picked.reshape(token_count * 2, specialist_index)
    busiest_specialist = favored_specialist[0]
    before = (jnp.cumsum(flat_routes, axis=0) - flat_routes).reshape(
        token_count, 2, specialist_index
    )
    ranking = jnp.sum(before * picked, axis=2)
    placement_ceiling = jnp.where(
        jnp.arange(specialist_index, dtype=jnp.int32) == busiest_specialist,
        PLACEMENT_MOST,
        allowed_placements,
    )
    keeping = ranking < jnp.sum(picked * placement_ceiling[None, None, :], axis=2)
    row_total = question_vectors.shape[0]
    heads_out = attend(
        question_vectors.reshape(row_total, -1, HD),
        fresh_lookup_vectors.reshape(row_total, -1, HD),
        fresh_content_vectors.reshape(row_total, -1, HD),
        stored_lookup_sheets,
        stored_content_sheets,
        sequence_sheet_map,
        stored_position_counts,
    )
    own_attn = lax.psum_scatter(
        jnp.dot(heads_out, attention_merge_matrix, preferred_element_type=jnp.float32).astype(
            jnp.bfloat16
        ),
        "tensor",
        scatter_dimension=0,
        tiled=True,
    ).astype(jnp.float32)
    stream = (skip_stream_entry.astype(jnp.float32) + own_attn).astype(jnp.bfloat16)
    wide = stream.astype(jnp.float32)
    squares = jnp.mean(wide * wide, axis=1, keepdims=True)
    normed = (wide * lax.rsqrt(squares + 1e-05) * premix_scale_factor.astype(jnp.float32)).astype(
        jnp.bfloat16
    )
    main_slots = PLACEMENT_MOST
    table_main = slot_table(picked, ranking, keeping, main_slots)
    send = jnp.einsum(
        "nkes,nd->esd", table_main, normed, preferred_element_type=jnp.float32
    ).astype(jnp.bfloat16)
    expert_out = expert_pass(send, gating_matrices, expand_matrices, contract_matrices)
    chosen = jnp.einsum("nkes,esd->nkd", table_main, expert_out, preferred_element_type=jnp.float32)
    mixed = jnp.sum(selection_shares[:, :, None] * chosen, axis=1)
    return (wide + mixed).astype(jnp.bfloat16)


def solution(mesh):
    placed = (
        P(("dp", "expert", "tensor"), None),
        P(("dp", "expert"), "tensor"),
        P(("dp", "expert"), "tensor"),
        P(("dp", "expert"), "tensor"),
        P(("dp", "expert"), "tensor", None, None),
        P(("dp", "expert"), "tensor", None, None),
        P(("dp", "expert"), None),
        P(("dp", "expert")),
        P("tensor", None),
        P(),
        P(("dp", "expert", "tensor"), None),
        P(("dp", "expert", "tensor"), None),
        P(),
        P(),
        P("expert", ("dp", "tensor"), None),
        P("expert", ("dp", "tensor"), None),
        P("expert", ("dp", "tensor"), None),
    )
    return jax.shard_map(
        local,
        mesh=mesh,
        in_specs=placed,
        out_specs=P(("dp", "expert", "tensor"), None),
        check_vma=False,
    )
```

profile of v0, /device:TPU:1, one launch (start us, length us, event | category | flops | bytes accessed | tf_op | source)
XLA Modules:
  0.0 500.2 jit_solution(16697747358621664481)
XLA Ops:
  6.6 0.9 slice.44
  7.4 1.2 slice.49
  8.7 1.2 broadcast_compare_fusion.1
  9.8 0.7 compare_select_fusion
  10.5 1.3 slice_bitcast_fusion.5
  11.8 0.1 copy.32
  11.9 0.1 reshape.332
  12.0 1.3 slice_convert_fusion
  13.3 1.6 select_reduce_fusion.2
  14.8 8.8 %gather_fusion.1 = bf16[136,128,128]{2,1,0:T(8,128)(2,1)} fusion(bf16[40,128,128]{2,1,0:T(8,128)(2,1)} %bitcast.233, s32[1024]{0:T(1024)S(1)} %pad_clamp_fusion), kind=kCustom, calls=%fused_computation.1 | custom fusion | bytes 8913440 | tf_op jit(solution)/shard_map/gather | solution.py:37
  23.7 1.3 copy-done.2
  25.0 7.5 %gather_fusion = bf16[136,128,128]{2,1,0:T(8,128)(2,1)} fusion(bf16[40,128,128]{2,1,0:T(8,128)(2,1)S(1)} %bitcast.234, s32[1024]{0:T(1024)S(1)} %pad_clamp_fusion), kind=kCustom, calls=%fused_computation | custom fusion | bytes 8913440 | tf_op jit(solution)/shard_map/gather | solution.py:36
  32.6 0.8 copy-done.9
  33.4 1.7 select_reduce_fusion
  35.2 0.3 bitcast_reduce_fusion
  35.5 0.2 convolution_bitcast_fusion.2
  35.7 0.3 fusion.43
  36.1 0.1 broadcast_compare_fusion
  36.2 0.1 fusion.88
  36.4 1.3 select_reduce_fusion.1
  37.7 0.3 bitcast_reduce_fusion.1
  38.0 1.4 slice-done.2
  39.4 0.8 fusion.45
  40.1 1.6 convolution_convert_fusion
  41.9 0.1 copy.38
  42.0 0.1 eq.56
  42.0 0.1 fusion.82
  42.8 0.1 reduce_window_sum.11
  42.8 0.2 select_reduce_fusion.3
  43.0 0.1 reduce_sum.82
  43.1 0.1 copy.39
  43.2 0.1 select_reduce_fusion.4
  43.4 24.8 %reduce-scatter.5.cloned.1.call-done = bf16[16,4096]{1,0:T(8,128)(2,1)} async-done(((bf16[64,4096]{1,0:T(8,128)(2,1)}), bf16[16,4096]{1,0:T(8,128)(2,1)}) %reduce-scatter.5.cloned.1.call-update) | async-done | bytes 131088 | tf_op jit(solution)/shard_map/reduce_scatter | solution.py:190
  68.1 1.1 fusion.53
  69.2 1.2 fusion.5
  70.4 0.2 copy.41
  70.6 15.7 %all_to_all.10 = bf16[8,1,6,4096]{3,2,1,0:T(8,128)(2,1)S(1)} all-to-all(bf16[8,1,6,4096]{3,2,1,0:T(8,128)(2,1)S(1)} %copy.41), channel_id=1, replica_groups=mesh['dp'=8,'expert'=8,'tensor'=4] {'expert'}, dimensions={0} | all-to-all | bytes 786432 | tf_op jit(solution)/shard_map/all_to_all | solution.py:116
  86.4 1.0 copy.42
  87.4 0.2 reduce-scatter.7.cloned.1.call-start
  87.6 117.5 %all-gather.2.cloned.1.call-done = bf16[256,1,6,4096]{3,0,2,1:T(8,128)(2,1)} async-done(((bf16[8,1,6,4096]{3,0,2,1:T(8,128)(2,1)}), bf16[256,1,6,4096]{3,0,2,1:T(8,128)(2,1)}) %all-gather.2.cloned.1.call-update) | async-done | bytes 12582928 | tf_op jit(solution)/shard_map/all_gather | solution.py:123
  205.1 7.5 %fusion.9 = f32[256,1,6,224]{0,3,2,1:T(8,128)S(1)} fusion(bf16[1,224,4096]{2,1,0:T(8,128)(2,1)} %param.31, bf16[256,1,6,4096]{3,0,2,1:T(8,128)(2,1)} %all-gather.2.cloned.1.call-done), kind=kOutput, calls=%fused_computation.15 | convolution fusion | flops 2818572288 | bytes 15794176 | tf_op jit(solution)/shard_map/qesd,efd->qesf/dot_general | solution.py:124
  212.6 19.3 %fusion.97 = bf16[32,8,6,4096]{3,1,0,2:T(8,128)(2,1)} fusion(bf16[1,224,4096]{2,1,0:T(8,128)(2,1)S(1)} %copy-done, bf16[1,224,4096]{2,1,0:T(8,128)(2,1)} %param.32, bf16[256,1,6,4096]{3,0,2,1:T(8,128)(2,1)} %all-gather.2.cloned.1.call-done, f32[256,1,6,224]{0,3,2,1:T(8,128)S(1)} %fusion.9), kind=kOutput, calls=%fused_computation.124 | convolution fusion | flops 5645500416 | bytes 30212096 | tf_op jit(solution)/shard_map/qesf,efd->qesd/dot_general | solution.py:132
  231.9 10.6 %copy.58 = bf16[32,8,6,4096]{3,1,2,0:T(8,128)(2,1)} copy(bf16[32,8,6,4096]{3,1,0,2:T(8,128)(2,1)} %fusion.97) | data formatting | bytes 25165824
  242.6 230.3 %reduce-scatter.7.cloned.1.call-done = bf16[8,24576]{1,0:T(8,128)(2,1)} async-done(((bf16[256,24576]{1,0:T(8,128)(2,1)}), bf16[8,24576]{1,0:T(8,128)(2,1)}) %reduce-scatter.7.cloned.1.call-update) | async-done | bytes 393232
  472.9 1.2 copy.43
  474.1 18.4 %all_to_all.11 = bf16[8,1,6,4096]{3,2,1,0:T(8,128)(2,1)S(1)} all-to-all(bf16[8,1,6,4096]{3,2,1,0:T(8,128)(2,1)S(1)} %copy.43), channel_id=1, replica_groups=mesh['dp'=8,'expert'=8,'tensor'=4] {'expert'}, dimensions={0} | all-to-all | bytes 786432 | tf_op jit(solution)/shard_map/all_to_all | solution.py:139
  492.6 0.3 fusion.39
  492.9 0.7 fusion.56
  (65 shorter events, 0.4 us)
Async XLA Ops:
  6.5 206.1 %copy-start = (bf16[1,224,4096]{2,1,0:T(8,128)(2,1)S(1)}, bf16[1,224,4096]{2,1,0:T(8,128)(2,1)}, u32[]{:S(2)}) copy-start(bf16[1,224,4096]{2,1,0:T(8,128)(2,1)} %param.33) | copy-start | bytes 5505028
  6.5 61.6 %reduce-scatter.5.cloned.1.call-start = ((), (), s32[]{:S(2)}) async-start(), calls=%async_computation.4 | async-start | bytes 655360 | tf_op jit(solution)/shard_map/reduce_scatter | solution.py:190
  23.7 1.3 copy-start.2
  25.0 10.7 %slice-start = ((s8[4456448]{0:T(1024)(128)(4,1)}), s8[262144]{0:T(1024)(128)(4,1)S(1)}, s32[]{:S(2)}) async-start(s8[4456448]{0:T(1024)(128)(4,1)} %bitcast.229), calls=%async_computation.7 | async-start | bytes 524288
  32.5 0.8 copy-start.9
  32.5 0.8 copy-start.13
  32.6 2.6 copy-start.11
  32.6 2.9 copy-start.14
  32.6 3.1 slice-start.1
  33.4 2.7 copy-start.15
  33.4 2.8 copy-start.10
  33.4 3.0 slice-start.3
  35.7 3.6 slice-start.2
  35.7 3.6 copy-start.8
  36.4 3.8 copy-start.3
  39.3 2.5 copy-start.6
  39.3 3.8 copy-start.7
  39.3 3.8 copy-start.16
  39.4 28.8 %copy-start.4 = (bf16[16,4096]{1,0:T(8,128)(2,1)S(1)}, bf16[16,4096]{1,0:T(8,128)(2,1)}, u32[]{:S(2)}) copy-start(bf16[16,4096]{1,0:T(8,128)(2,1)} %param.17) | copy-start | bytes 393220
  41.8 163.3 %all-gather.2.cloned.1.call-start = ((), (), s32[]{:S(2)}) async-start(), calls=%async_computation.5 | async-start | bytes 12976128 | tf_op jit(solution)/shard_map/all_gather | solution.py:123
  87.4 385.5 %reduce-scatter.7.cloned.1.call-start = ((), (), s32[]{:S(2)}) async-start(), calls=%async_computation.6 | async-start | bytes 12976128
  242.5 250.0 %copy-start.12 = (f32[16,2]{0,1:T(2,128)S(1)}, f32[16,2]{0,1:T(2,128)}, u32[]{:S(2)}) copy-start(f32[16,2]{0,1:T(2,128)} %param.28) | copy-start | bytes 388
  242.5 250.4 %copy-start.5 = (bf16[16,4096]{1,0:T(8,128)(2,1)S(1)}, bf16[16,4096]{1,0:T(8,128)(2,1)}, u32[]{:S(2)}) copy-start(bf16[16,4096]{1,0:T(8,128)(2,1)} %reduce-scatter.5.cloned.1.call-done) | copy-start | bytes 393220
  242.6 251.1 %copy-start.1 = (bf16[1,224,4096]{2,1,0:T(8,128)(2,1)S(1)}, bf16[1,224,4096]{2,1,0:T(8,128)(2,1)}, u32[]{:S(2)}) copy-start(bf16[1,224,4096]{2,1,0:T(8,128)(2,1)} %param.33) | copy-start | bytes 5505028
Sparse Core Ops, SparseCore 0:
  41.9 26.1 reduce-scatter.4
  87.5 117.5 all-gather.1
  242.7 230.1 reduce-scatter.6
where the time goes:
time: 501 us; the launch traced here: 500 us
  waiting for transfers between devices  373 us (74%)
  local copies, waits for them, and re-layouts  36.9 us (7%)
  matrix products  35.9 us (7%)
  blocking collectives  34.2 us (7%)
  between operations  14.1 us (3%)
  other arithmetic  6.11 us (1%)
    unnamed x4, waiting for transfers between devices  230 us
    all_gather x1, waiting for transfers between devices, expert_pass(): row_piece = lax.all_gather(arrived, ('dp', 'tensor'), axis=0, tiled=True)  118 us
    reduce_scatter x1, waiting for transfers between devices, local(): lax.psum_scatter(jnp.dot(heads_out, attention_merge_matrix, preferred_ele...  24.8 us
    dot_general x1, matrix products, expert_pass(): jnp.einsum('qesf,efd->qesd', hidden, contract_matrices, preferred_element...  19.3 us
    all_to_all x1, blocking collectives, expert_pass(): lax.all_to_all(summed, 'expert', split_axis=0, concat_axis=0, tiled=True)  18.4 us
    all_to_all x1, blocking collectives, expert_pass(): lax.all_to_all(send.reshape(holders, local_count, slot_count, model_width...  15.7 us
    unnamed x42, local copies, waits for them, and re-layouts  12.9 us
  transfers between devices with their start and end apart: 3, of which 3 were waited for; matrix products, arithmetic and copies ran while one was open for 0% of the time, Pallas kernels for 0%

commit v1 on v0

--- a/solution.py
+++ b/solution.py
@@ -120,7 +120,12 @@
         concat_axis=0,
         tiled=True,
     )
-    row_piece = lax.all_gather(arrived, ("dp", "tensor"), axis=0, tiled=True)
+    row_piece = jnp.concatenate(
+        lax.all_to_all(
+            jnp.stack([arrived] * lax.axis_size(("dp", "tensor"))), ("dp", "tensor"), 0, 0
+        ),
+        axis=0,
+    )
     gate_part = jnp.einsum(
         "qesd,efd->qesf", row_piece, gating_matrices, preferred_element_type=jnp.float32
     )

time: 501 us -> 671 us (1.34)
  blocking collectives: 34.2 us -> 315 us
  waiting for transfers between devices: 373 us -> 256 us
  local copies, waits for them, and re-layouts: 36.9 us -> 46.8 us
    all_to_all x0 -> x1, blocking collectives: none -> 281 us  [expert_pass(): lax.all_to_all(jnp.stack([arrived] * lax.axis_size(('dp', 'tensor'))), ('...]
    all_gather x1 -> x0, waiting for transfers between devices: 118 us -> none  [expert_pass(): row_piece = lax.all_gather(arrived, ('dp', 'tensor'), axis=0, tiled=True)]
    unnamed x42 -> x46, local copies, waits for them, and re-layouts: 12.9 us -> 17.4 us
    unnamed x4 -> x3, waiting for transfers between devices: 230 us -> 231 us
  transfers between devices with their start and end apart: 3 -> 2, of which waited for: 3 -> 2; matrix products, arithmetic and copies ran while one was open for 0% -> 0% of each run, Pallas kernels for 0% -> 0%
where the time goes in v1:
time: 671 us; the launch traced here: 670 us
  blocking collectives  315 us (47%)
  waiting for transfers between devices  256 us (38%)
  local copies, waits for them, and re-layouts  46.8 us (7%)
  matrix products  32.4 us (5%)
  between operations  14.4 us (2%)
    all_to_all x1, blocking collectives, expert_pass(): lax.all_to_all(jnp.stack([arrived] * lax.axis_size(('dp', 'tensor'))), ('...  281 us
    unnamed x3, waiting for transfers between devices  231 us
    reduce_scatter x1, waiting for transfers between devices, local(): lax.psum_scatter(jnp.dot(heads_out, attention_merge_matrix, preferred_ele...  24.8 us
    dot_general x1, matrix products, expert_pass(): jnp.einsum('qesf,efd->qesd', hidden, contract_matrices, preferred_element...  19.4 us
    all_to_all x1, blocking collectives, expert_pass(): lax.all_to_all(summed, 'expert', split_axis=0, concat_axis=0, tiled=True)  18.3 us
    unnamed x46, local copies, waits for them, and re-layouts  17.4 us
    all_to_all x1, blocking collectives, expert_pass(): lax.all_to_all(send.reshape(holders, local_count, slot_count, model_width...  15.7 us
  transfers between devices with their start and end apart: 2, of which 2 were waited for; matrix products, arithmetic and copies ran while one was open for 0% of the time, Pallas kernels for 0%

profile of v1, /device:TPU:1, one launch (start us, length us, event | category | flops | bytes accessed | tf_op | source)
XLA Modules:
  0.0 670.5 jit_solution(5575072553941243543)
XLA Ops:
  6.6 0.9 slice.44
  7.4 1.2 slice.49
  8.7 1.2 broadcast_compare_fusion.1
  9.8 0.7 compare_select_fusion
  10.5 1.3 slice_bitcast_fusion.5
  11.8 0.1 copy.32
  11.9 0.1 reshape.338
  12.0 1.3 slice_convert_fusion
  13.3 1.6 select_reduce_fusion.2
  14.8 8.8 %gather_fusion.1 = bf16[136,128,128]{2,1,0:T(8,128)(2,1)} fusion(bf16[40,128,128]{2,1,0:T(8,128)(2,1)} %bitcast.234, s32[1024]{0:T(1024)S(1)} %pad_clamp_fusion), kind=kCustom, calls=%fused_computation.1 | custom fusion | bytes 8913440 | tf_op jit(solution)/shard_map/gather | solution.py:37
  23.7 1.3 copy-done.2
  25.0 7.5 %gather_fusion = bf16[136,128,128]{2,1,0:T(8,128)(2,1)} fusion(bf16[40,128,128]{2,1,0:T(8,128)(2,1)S(1)} %bitcast.235, s32[1024]{0:T(1024)S(1)} %pad_clamp_fusion), kind=kCustom, calls=%fused_computation | custom fusion | bytes 8913440 | tf_op jit(solution)/shard_map/gather | solution.py:36
  32.6 0.8 copy-done.10
  33.4 1.7 select_reduce_fusion
  35.2 0.3 bitcast_reduce_fusion
  35.5 0.2 convolution_bitcast_fusion.2
  35.7 0.3 fusion.41
  36.1 0.1 broadcast_compare_fusion
  36.2 0.1 fusion.89
  36.4 1.3 select_reduce_fusion.1
  37.7 0.3 bitcast_reduce_fusion.1
  38.0 1.4 slice-done.2
  39.4 0.8 fusion.43
  40.1 1.6 convolution_convert_fusion
  41.9 0.1 copy.38
  42.0 0.1 eq.56
  42.0 0.1 fusion.83
  42.8 0.2 select_reduce_fusion.3
  43.0 0.1 reduce_sum.82
  43.1 0.1 copy.39
  43.2 0.1 select_reduce_fusion.4
  43.4 24.8 %reduce-scatter.5.cloned.1.call-done = bf16[16,4096]{1,0:T(8,128)(2,1)} async-done(((bf16[64,4096]{1,0:T(8,128)(2,1)}), bf16[16,4096]{1,0:T(8,128)(2,1)}) %reduce-scatter.5.cloned.1.call-update) | async-done | bytes 131088 | tf_op jit(solution)/shard_map/reduce_scatter | solution.py:195
  68.1 1.1 fusion.50
  69.2 1.2 fusion.7
  70.4 0.2 copy.41
  70.6 15.7 %all_to_all.18 = bf16[8,1,6,4096]{3,2,1,0:T(8,128)(2,1)S(1)} all-to-all(bf16[8,1,6,4096]{3,2,1,0:T(8,128)(2,1)S(1)} %copy.41), channel_id=1, replica_groups=mesh['dp'=8,'expert'=8,'tensor'=4] {'expert'}, dimensions={0} | all-to-all | bytes 786432 | tf_op jit(solution)/shard_map/all_to_all | solution.py:116
  86.4 0.2 copy.42
  86.6 6.2 stack.2
  92.8 281.1 %all_to_all.19 = bf16[32,8,1,6,4096]{4,1,3,2,0:T(8,128)(2,1)S(1)} all-to-all(bf16[32,8,1,6,4096]{4,1,3,2,0:T(8,128)(2,1)} %stack.2), channel_id=1, replica_groups=mesh['dp'=8,'expert'=8,'tensor'=4] {'dp','tensor'}, dimensions={0} | all-to-all | bytes 25165824 | tf_op jit(solution)/shard_map/all_to_all | solution.py:124
  373.8 4.5 copy-done.3
  378.3 3.8 fusion.11
  382.1 19.4 %fusion.98 = bf16[32,8,6,4096]{3,1,0,2:T(8,128)(2,1)} fusion(bf16[1,224,4096]{2,1,0:T(8,128)(2,1)S(1)} %copy-done, bf16[1,224,4096]{2,1,0:T(8,128)(2,1)} %param.32, bf16[32,8,1,6,4096]{4,1,3,2,0:T(8,128)(2,1)} %copy-done.3, f32[256,1,6,224]{0,3,2,1:T(8,128)S(1)} %fusion.11), kind=kOutput, calls=%fused_computation.125 | convolution fusion | flops 5645500416 | bytes 30212096 | tf_op jit(solution)/shard_map/qesf,efd->qesd/dot_general | solution.py:137
  401.6 10.6 %copy.59 = bf16[32,8,6,4096]{3,1,2,0:T(8,128)(2,1)} copy(bf16[32,8,6,4096]{3,1,0,2:T(8,128)(2,1)} %fusion.98) | data formatting | bytes 25165824
  412.2 230.8 %reduce-scatter.7.cloned.1.call-done = bf16[8,24576]{1,0:T(8,128)(2,1)} async-done(((bf16[256,24576]{1,0:T(8,128)(2,1)}), bf16[8,24576]{1,0:T(8,128)(2,1)}) %reduce-scatter.7.cloned.1.call-update) | async-done | bytes 393232
  643.0 1.2 copy.44
  644.3 18.3 %all_to_all.20 = bf16[8,1,6,4096]{3,2,1,0:T(8,128)(2,1)S(1)} all-to-all(bf16[8,1,6,4096]{3,2,1,0:T(8,128)(2,1)S(1)} %copy.44), channel_id=1, replica_groups=mesh['dp'=8,'expert'=8,'tensor'=4] {'expert'}, dimensions={0} | all-to-all | bytes 786432 | tf_op jit(solution)/shard_map/all_to_all | solution.py:144
  662.6 0.3 fusion.37
  663.0 0.7 fusion.53
  (68 shorter events, 0.4 us)
Async XLA Ops:
  6.5 375.6 %copy-start = (bf16[1,224,4096]{2,1,0:T(8,128)(2,1)S(1)}, bf16[1,224,4096]{2,1,0:T(8,128)(2,1)}, u32[]{:S(2)}) copy-start(bf16[1,224,4096]{2,1,0:T(8,128)(2,1)} %param.33) | copy-start | bytes 5505028
  6.5 61.6 %reduce-scatter.5.cloned.1.call-start = ((), (), s32[]{:S(2)}) async-start(), calls=%async_computation.5 | async-start | bytes 655360 | tf_op jit(solution)/shard_map/reduce_scatter | solution.py:195
  23.7 1.3 copy-start.2
  25.0 10.7 %slice-start = ((s8[4456448]{0:T(1024)(128)(4,1)}), s8[262144]{0:T(1024)(128)(4,1)S(1)}, s32[]{:S(2)}) async-start(s8[4456448]{0:T(1024)(128)(4,1)} %bitcast.230), calls=%async_computation.7 | async-start | bytes 524288
  32.5 0.8 copy-start.10
  32.5 0.8 copy-start.14
  32.6 2.6 copy-start.12
  32.6 2.9 copy-start.15
  32.6 3.1 slice-start.1
  33.4 2.7 copy-start.16
  33.4 2.8 copy-start.11
  33.4 3.0 slice-start.3
  35.7 3.6 slice-start.2
  35.7 3.6 copy-start.9
  36.4 3.8 copy-start.4
  39.3 2.5 copy-start.7
  39.3 3.8 copy-start.8
  39.3 3.8 copy-start.18
  39.4 28.8 %copy-start.5 = (bf16[16,4096]{1,0:T(8,128)(2,1)S(1)}, bf16[16,4096]{1,0:T(8,128)(2,1)}, u32[]{:S(2)}) copy-start(bf16[16,4096]{1,0:T(8,128)(2,1)} %param.17) | copy-start | bytes 393220
  41.8 601.2 %reduce-scatter.7.cloned.1.call-start = ((), (), s32[]{:S(2)}) async-start(), calls=%async_computation.6 | async-start | bytes 12976128
  92.8 285.5 %copy-start.17 = (bf16[1,224,4096]{2,1,0:T(8,128)(2,1)S(1)}, bf16[1,224,4096]{2,1,0:T(8,128)(2,1)}, u32[]{:S(2)}) copy-start(bf16[1,224,4096]{2,1,0:T(8,128)(2,1)} %param.31) | copy-start | bytes 5505028
  373.8 4.5 copy-start.3
  412.2 250.4 %copy-start.13 = (f32[16,2]{0,1:T(2,128)S(1)}, f32[16,2]{0,1:T(2,128)}, u32[]{:S(2)}) copy-start(f32[16,2]{0,1:T(2,128)} %param.28) | copy-start | bytes 388
  412.2 250.8 %copy-start.6 = (bf16[16,4096]{1,0:T(8,128)(2,1)S(1)}, bf16[16,4096]{1,0:T(8,128)(2,1)}, u32[]{:S(2)}) copy-start(bf16[16,4096]{1,0:T(8,128)(2,1)} %reduce-scatter.5.cloned.1.call-done) | copy-start | bytes 393220
  412.2 251.4 %copy-start.1 = (bf16[1,224,4096]{2,1,0:T(8,128)(2,1)S(1)}, bf16[1,224,4096]{2,1,0:T(8,128)(2,1)}, u32[]{:S(2)}) copy-start(bf16[1,224,4096]{2,1,0:T(8,128)(2,1)} %param.33) | copy-start | bytes 5505028
Sparse Core Ops, SparseCore 0:
  41.9 26.1 reduce-scatter.4
  412.3 230.6 reduce-scatter.6
